TPU v7x, 256 devices: a whole 4x4x8 slice. The times are simulated.
256 devices in a mesh: row: 32 (over z, x), col: 4 (over y), rep: 2 (over core).
Axes of the slice: x: 4, y: 4, z: 8, core: 2. Of those that a mesh axis runs over, the one named last changes fastest.
Arguments:
- amplitudes: bfloat16 [32768, 8192], P('row', ('rep', 'col')), may hold values from -6 to 6
- integrals: bfloat16 [8192, 4096], P(('rep', 'row'), 'col'), may hold values from -0.1875 to 0.1875
- tile_mask: int32 [64, 32], replicated, may hold values from 0 to 1
- k_irrep: int32 [64], replicated, may hold values from 0 to 3
- n_irrep: int32 [32], replicated, may hold values from 0 to 3
- stored_tile: int32 [64], replicated, may hold values from 0 to 63, as said below
Outputs:
- ladder: bfloat16 [32768, 4096], P('row', ('col', 'rep'))
Inputs may be any that keep to these rules, and one draw needn't show every extreme that they name: `stored_tile`: for each q, slots q * 32 to (q + 1) * 32 - 1 hold a permutation of the tiles q * 32 to (q + 1) * 32 - 1.
All inputs are finite; a program needn't handle non-finite values.
Results may differ from a plain program's by a relative error of at most 0.001.
Values may be sent and summed in bfloat16 or wider, within the bound.
No kernel may reach another device: no remote copies, remote signals or barrier semaphores. Data moves between devices by JAX's collectives and lax.ppermute only.
A program may use at most 128 MiB of HBM per device.

v0:
```python
import jax
import jax.numpy as jnp
from jax import lax
from jax.sharding import PartitionSpec as P

TS = 128


def on_device(amplitudes, integrals, tile_mask, k_irrep, n_irrep, stored_tile):
    slab = lax.axis_index("rep")
    column = lax.axis_index("col")
    ncol = integrals.shape[1]
    tiles_col = ncol // TS
    n_labels = lax.dynamic_slice_in_dim(n_irrep, column * tiles_col, tiles_col)
    mask_cols = lax.dynamic_slice_in_dim(tile_mask, column * tiles_col, tiles_col, 1)
    stored_rows = integrals.shape[0]
    kq = stored_rows * lax.axis_size("row")
    slab_tiles = kq // TS
    slots = lax.dynamic_slice_in_dim(stored_tile, slab * slab_tiles, slab_tiles)
    gathered = lax.all_gather(integrals, "row", axis=0, tiled=True)
    same = jnp.take(k_irrep, slots)[:, None] == n_labels[None, :]
    occupied = jnp.take(mask_cols, slots, axis=0) == 1
    weights = jnp.logical_and(same, occupied).astype(jnp.bfloat16)
    shaped = gathered.reshape(slab_tiles, TS, tiles_col, TS) * weights[:, None, :, None]
    masked = shaped.reshape(kq, ncol)
    amp_slab = lax.all_gather(amplitudes, "col", axis=1, tiled=True)
    mrow = amp_slab.shape[0]
    local_ids = slots - slab * slab_tiles
    ordered = jnp.take(amp_slab.reshape(mrow, slab_tiles, TS), local_ids, axis=1).reshape(mrow, kq)
    partial_value = jnp.dot(ordered, masked, preferred_element_type=jnp.float32)
    return lax.psum_scatter(partial_value, "rep", scatter_dimension=1, tiled=True).astype(
        jnp.bfloat16
    )


def solution(mesh):
    placed = (P("row", ("rep", "col")), P(("rep", "row"), "col"), P(), P(), P(), P())
    return jax.shard_map(
        on_device, mesh=mesh, in_specs=placed, out_specs=P("row", ("col", "rep")), check_vma=False
    )
```

profile of v0, /device:TPU:1, one launch (start us, length us, event | category | flops | bytes accessed | tf_op | source)
XLA Modules:
  0.0 242.3 jit_solution(16062950526228524270)
XLA Ops:
  6.5 0.0 copy-start
  6.5 0.0 all-gather.3.cloned.1.call-start
  6.5 3.9 %copy.13 = bf16[1024,1024]{0,1:T(8,128)(2,1)} copy(bf16[1024,1024]{1,0:T(8,128)(2,1)} %param.6) | data formatting | bytes 4194304 | tf_op args[0]
  10.5 0.0 all-gather.3.cloned.1.call-update
  10.5 0.0 all-gather.5.cloned.1.call-start
  10.6 0.7 all-gather.5.cloned.1.call-update
  11.3 0.0 reduce-scatter.2.cloned.1.call-start
  11.3 0.7 dynamic_slice.10
  12.0 0.0 copy-done
  12.0 0.1 copy.19
  12.1 0.7 compare_and_fusion
  12.9 1.4 gather_fusion.1
  14.2 0.6 gather_fusion.2
  14.8 0.1 copy.17
  14.9 0.1 fusion.3
  15.0 0.1 copy.18
  15.1 0.1 broadcast_bitcast_fusion
  15.1 84.8 %all-gather.3.cloned.1.call-done = bf16[1024,4096]{0,1:T(8,128)(2,1)} async-done(((bf16[1024,1024]{0,1:T(8,128)(2,1)}), bf16[1024,4096]{0,1:T(8,128)(2,1)}) %all-gather.3.cloned.1.call-update) | async-done | bytes 8388624 | tf_op jit(solution)/shard_map/all_gather | solution.py:26
  99.9 12.0 %copy.14 = bf16[1024,32,128]{2,0,1:T(8,128)(2,1)} copy(bf16[1024,32,128]{0,2,1:T(8,128)(2,1)} %bitcast.14) | data formatting | bytes 16777216 | tf_op jit(solution)/shard_map/reshape | solution.py:29
  111.9 8.4 %gather_fusion = bf16[32,1024,128]{2,1,0:T(8,128)(2,1)} fusion(bf16[1024,32,128]{2,0,1:T(8,128)(2,1)} %copy.14, s32[1024]{0:T(1024)S(1)} %pad_clamp_fusion.1), kind=kCustom, calls=%fused_computation | custom fusion | bytes 16777344 | tf_op jit(solution)/shard_map/jit(_take)/gather | solution.py:29
  120.3 12.0 %copy.15 = bf16[1024,32,128]{0,2,1:T(8,128)(2,1)} copy(bf16[1024,32,128]{2,0,1:T(8,128)(2,1)} %bitcast.12) | data formatting | bytes 16777216 | tf_op jit(solution)/shard_map/jit(_take)/gather | solution.py:29
  132.3 7.3 %bitcast_select_fusion = bf16[1024,4096]{0,1:T(8,128)(2,1)} fusion(bf16[1024,32,128]{0,2,1:T(8,128)(2,1)} %copy.15, pred[4096]{0:T(1024)(128)(4,1)S(1)} %broadcast_bitcast_fusion), kind=kLoop, calls=%fused_computation.6 | loop fusion | flops 4194304 | bytes 16781312 | tf_op jit(solution)/shard_map/jit(_take)/select_n | solution.py:29
  139.6 61.2 %all-gather.5.cloned.1.call-done = bf16[4096,1024]{1,0:T(8,128)(2,1)} async-done(((bf16[128,1024]{1,0:T(8,128)(2,1)}), bf16[4096,1024]{1,0:T(8,128)(2,1)}) %all-gather.5.cloned.1.call-update) | async-done | bytes 8388624 | tf_op jit(solution)/shard_map/all_gather | solution.py:20
  200.8 0.0 copy-start.2
  200.8 1.1 mul.21
  201.9 2.2 copy-done.2
  204.2 0.0 copy-start.1
  204.2 13.0 %fusion = f32[1024,1024]{1,0:T(8,128)} fusion(bf16[1024,4096]{0,1:T(8,128)(2,1)S(1)} %copy-done.2, bf16[4096,1024]{1,0:T(8,128)(2,1)} %all-gather.5.cloned.1.call-done, bf16[512,8,8,128]{3,2,1,0:T(8,128)(2,1)S(1)} %bitcast.13), kind=kOutput, calls=%fused_computation.4 | convolution fusion | flops 8594128896 | bytes 29360128 | tf_op jit(solution)/shard_map/dot_general | solution.py:30
  217.1 0.0 reduce-scatter.2.cloned.1.call-update
  217.1 16.0 %reduce-scatter.2.cloned.1.call-done = f32[1024,512]{1,0:T(8,128)} async-done(((f32[1024,1024]{1,0:T(8,128)}), f32[1024,512]{1,0:T(8,128)}) %reduce-scatter.2.cloned.1.call-update) | async-done | bytes 2097168 | tf_op jit(solution)/shard_map/reduce_scatter | solution.py:31
  233.1 2.7 %convert_element_type.11 = bf16[1024,512]{1,0:T(8,128)(2,1)} convert(f32[1024,512]{1,0:T(8,128)} %reduce-scatter.2.cloned.1.call-done) | non-fusion elementwise | flops 524288 | bytes 3145728 | tf_op jit(solution)/shard_map/convert_element_type | solution.py:31
  235.8 0.0 copy-done.1
  (4 shorter events, 0.0 us)
Async XLA Ops:
  6.5 5.5 %copy-start = (s32[64,32]{0,1:T(8,128)S(1)}, s32[64,32]{0,1:T(8,128)}, u32[]{:S(2)}) copy-start(s32[64,32]{0,1:T(8,128)} %param.8) | copy-start | bytes 24580
  6.5 93.4 %all-gather.3.cloned.1.call-start = ((), (), s32[]{:S(2)}) async-start(), calls=%async_computation.1 | async-start | bytes 10485760 | tf_op jit(solution)/shard_map/all_gather | solution.py:26
  10.5 190.3 %all-gather.5.cloned.1.call-start = ((), (), s32[]{:S(2)}) async-start(), calls=%async_computation.2 | async-start | bytes 8650752 | tf_op jit(solution)/shard_map/all_gather | solution.py:20
  11.3 221.9 %reduce-scatter.2.cloned.1.call-start = ((), (), s32[]{:S(2)}) async-start(), calls=%async_computation.3 | async-start | bytes 6291456 | tf_op jit(solution)/shard_map/reduce_scatter | solution.py:31
  200.8 3.4 %copy-start.2 = (bf16[1024,4096]{0,1:T(8,128)(2,1)S(1)}, bf16[1024,4096]{0,1:T(8,128)(2,1)}, u32[]{:S(2)}) copy-start(bf16[1024,4096]{0,1:T(8,128)(2,1)} %bitcast_select_fusion) | copy-start | bytes 25165828
  204.2 31.7 %copy-start.1 = (s32[64,32]{0,1:T(8,128)S(1)}, s32[64,32]{0,1:T(8,128)}, u32[]{:S(2)}) copy-start(s32[64,32]{0,1:T(8,128)} %param.8) | copy-start | bytes 24580
Sparse Core Ops, SparseCore 0:
  10.6 89.2 all-gather.2
  102.5 98.2 all-gather.4
  217.3 15.8 reduce-scatter.1
where the time goes:
time: 243 us; the launch traced here: 242 us
  waiting for transfers between devices  163 us (67%)
  local copies, waits for them, and re-layouts  42.7 us (18%)
  between operations  13.1 us (5%)
  matrix products  13 us (5%)
  other arithmetic  10.8 us (4%)
    all_gather x1, waiting for transfers between devices, on_device(): amp_slab = lax.all_gather(amplitudes, 'col', axis=1, tiled=True)  84.8 us
    all_gather x1, waiting for transfers between devices, on_device(): gathered = lax.all_gather(integrals, 'row', axis=0, tiled=True)  61.2 us
    gather x2, local copies, waits for them, and re-layouts, on_device(): jnp.take(amp_slab.reshape(mrow, slab_tiles, TS), local_ids, axis=1)  20.4 us
    reduce_scatter x1, waiting for transfers between devices, on_device(): lax.psum_scatter(partial_value, 'rep', scatter_dimension=1, tiled=True)  16 us
    dot_general x1, matrix products, on_device(): partial_value = jnp.dot(ordered, masked, preferred_element_type=jnp.float32)  13 us
    reshape x1, local copies, waits for them, and re-layouts, on_device(): amp_slab.reshape(mrow, slab_tiles, TS)  12 us
    select_n x1, other arithmetic, on_device(): jnp.take(amp_slab.reshape(mrow, slab_tiles, TS), local_ids, axis=1)  7.27 us
    unnamed x8, local copies, waits for them, and re-layouts  6.26 us
  transfers between devices with their start and end apart: 3, of which 3 were waited for; matrix products, arithmetic and copies ran while one was open for 18% of the time, Pallas kernels for 0%

commit v1 on v0

--- a/solution.py
+++ b/solution.py
@@ -2,11 +2,38 @@
 import jax.numpy as jnp
 from jax import lax
 from jax.sharding import PartitionSpec as P
+from jax.lax import axis_index, ppermute, psum
 
 TS = 128
 
 
 def on_device(amplitudes, integrals, tile_mask, k_irrep, n_irrep, stored_tile):
+
+    def switch_weights_by_axis(xs):
+        v_now, vec_out, plain = (psum(1, "col"), axis_index("col"), xs.shape[1])
+        side_arr = lax.dynamic_update_slice_in_dim(
+            jnp.zeros(
+                [i0 * v_now if to_i == 1 else i0 for to_i, i0 in enumerate(xs.shape)], xs.dtype
+            ),
+            xs,
+            vec_out * plain,
+            axis=1,
+        )
+        newest = oldest = xs
+        for dd in range(1, v_now // 2 + 1):
+            newest = ppermute(newest, "col", [(to_i, (to_i + 1) % v_now) for to_i in range(v_now)])
+            side_arr = lax.dynamic_update_slice_in_dim(
+                side_arr, newest, (vec_out - dd) % v_now * plain, axis=1
+            )
+            if 2 * dd < v_now:
+                oldest = ppermute(
+                    oldest, "col", [(to_i, (to_i - 1) % v_now) for to_i in range(v_now)]
+                )
+                side_arr = lax.dynamic_update_slice_in_dim(
+                    side_arr, oldest, (vec_out + dd) % v_now * plain, axis=1
+                )
+        return side_arr
+
     slab = lax.axis_index("rep")
     column = lax.axis_index("col")
     ncol = integrals.shape[1]
@@ -23,7 +50,7 @@
     weights = jnp.logical_and(same, occupied).astype(jnp.bfloat16)
     shaped = gathered.reshape(slab_tiles, TS, tiles_col, TS) * weights[:, None, :, None]
     masked = shaped.reshape(kq, ncol)
-    amp_slab = lax.all_gather(amplitudes, "col", axis=1, tiled=True)
+    amp_slab = switch_weights_by_axis(amplitudes)
     mrow = amp_slab.shape[0]
     local_ids = slots - slab * slab_tiles
     ordered = jnp.take(amp_slab.reshape(mrow, slab_tiles, TS), local_ids, axis=1).reshape(mrow, kq)

time: 243 us -> 196 us (0.81)
  waiting for transfers between devices: 163 us -> 95.9 us
  local copies, waits for them, and re-layouts: 42.7 us -> 56.3 us
  starting transfers between devices: 0.08 us -> 5.29 us
    all_gather x1 -> x0, waiting for transfers between devices: 84.8 us -> none  [on_device(): amp_slab = lax.all_gather(amplitudes, 'col', axis=1, tiled=True)]
    ppermute x0 -> x3, waiting for transfers between devices: none -> 72.4 us  [the longest x2 72.4 us: switch_weights_by_axis(): ppermute(newest, 'col', [(to_i, (to_i + 1) % v_now) for to_i in range(v_n...]
    all_gather x1, waiting for transfers between devices: 61.2 us -> 0.01 us  [on_device(): gathered = lax.all_gather(integrals, 'row', axis=0, tiled=True)]
    dynamic_update_slice x0 -> x4, local copies, waits for them, and re-layouts: none -> 10.8 us  [the longest x2 6.19 us: switch_weights_by_axis(): lax.dynamic_update_slice_in_dim(side_arr, newest, (vec_out - dd) % v_now...]
    reduce_scatter x1, waiting for transfers between devices: 16 us -> 22.8 us  [on_device(): lax.psum_scatter(partial_value, 'rep', scatter_dimension=1, tiled=True)]
    ppermute x0 -> x3, starting transfers between devices: none -> 5.25 us  [the longest x2 3.72 us: switch_weights_by_axis(): ppermute(newest, 'col', [(to_i, (to_i + 1) % v_now) for to_i in range(v_n...]
    broadcast_in_dim x0 -> x1, local copies, waits for them, and re-layouts: none -> 4.38 us  [switch_weights_by_axis(): jnp.zeros([i0 * v_now if to_i == 1 else i0 for to_i, i0 in enumerate(xs.s...]
  transfers between devices with their start and end apart: 3 -> 5, of which waited for: 3 -> 3; matrix products, arithmetic and copies ran while one was open for 18% -> 31% of each run, Pallas kernels for 0% -> 0%
where the time goes in v1:
time: 196 us; the launch traced here: 195 us
  waiting for transfers between devices  95.9 us (49%)
  local copies, waits for them, and re-layouts  56.3 us (29%)
  between operations  13.4 us (7%)
  matrix products  12.9 us (7%)
  other arithmetic  10.8 us (6%)
  starting transfers between devices  5.29 us (3%)
    ppermute x2, waiting for transfers between devices, switch_weights_by_axis(): ppermute(newest, 'col', [(to_i, (to_i + 1) % v_now) for to_i in range(v_n...  72.4 us
    reduce_scatter x1, waiting for transfers between devices, on_device(): lax.psum_scatter(partial_value, 'rep', scatter_dimension=1, tiled=True)  22.8 us
    gather x2, local copies, waits for them, and re-layouts, on_device(): jnp.take(amp_slab.reshape(mrow, slab_tiles, TS), local_ids, axis=1)  20.2 us
    dot_general x1, matrix products, on_device(): partial_value = jnp.dot(ordered, masked, preferred_element_type=jnp.float32)  12.9 us
    reshape x1, local copies, waits for them, and re-layouts, on_device(): amp_slab.reshape(mrow, slab_tiles, TS)  11.7 us
    select_n x1, other arithmetic, on_device(): jnp.take(amp_slab.reshape(mrow, slab_tiles, TS), local_ids, axis=1)  7.29 us
    dynamic_update_slice x2, local copies, waits for them, and re-layouts, switch_weights_by_axis(): lax.dynamic_update_slice_in_dim(side_arr, newest, (vec_out - dd) % v_now...  6.19 us
    unnamed x8, local copies, waits for them, and re-layouts  5.19 us
  transfers between devices with their start and end apart: 5, of which 3 were waited for; matrix products, arithmetic and copies ran while one was open for 31% of the time, Pallas kernels for 0%

profile of v1, /device:TPU:1, one launch (start us, length us, event | category | flops | bytes accessed | tf_op | source)
XLA Modules:
  0.0 194.7 jit_solution(16962613610249732498)
XLA Ops:
  6.5 0.0 copy-start
  6.5 0.0 all-gather.2.cloned.1.call-start
  6.5 0.7 all-gather.2.cloned.1.call-update
  7.3 0.0 reduce-scatter.2.cloned.1.call-start
  7.3 2.9 %copy.15 = bf16[1024,1024]{0,1:T(8,128)(2,1)S(1)} copy(bf16[1024,1024]{1,0:T(8,128)(2,1)} %param.6) | data formatting | bytes 4194304 | tf_op args[0]
  10.2 2.2 %collective-permute-start = (bf16[1024,1024]{0,1:T(8,128)(2,1)S(1)}, bf16[1024,1024]{0,1:T(8,128)(2,1)}, u32[]{:S(2)}, u32[]{:S(2)}) collective-permute-start(bf16[1024,1024]{0,1:T(8,128)(2,1)S(1)} %copy.15), channel_id=1, source_target_pairs={{0,2},{2,4},{4,6},{6,0},{1,3},{3,5},{5,7},{7,1},{8,10},{10,12},{12... | collective-permute-start | bytes 6291464 | tf_op jit(solution)/shard_map/ppermute | solution.py:24
  12.4 1.5 collective-permute-start.1
  13.9 43.4 %collective-permute-done = bf16[1024,1024]{0,1:T(8,128)(2,1)} collective-permute-done((bf16[1024,1024]{0,1:T(8,128)(2,1)S(1)}, bf16[1024,1024]{0,1:T(8,128)(2,1)}, u32[]{:S(2)}, u32[]{:S(2)}) %collective-permute-start) | collective-permute-done | bytes 2097184 | tf_op jit(solution)/shard_map/ppermute | solution.py:24
  57.3 1.5 collective-permute-start.2
  58.8 0.0 copy-done
  58.9 0.1 copy.23
  58.9 0.7 compare_and_fusion
  59.7 0.6 gather_fusion.2
  60.3 0.1 copy.21
  60.3 1.4 gather_fusion.1
  61.7 0.7 dynamic_slice.10
  62.4 0.1 fusion.3
  62.5 0.1 copy.22
  62.6 4.4 %broadcast_in_dim.43 = bf16[1024,4096]{0,1:T(8,128)(2,1)} broadcast(bf16[]{:T(256)} %constant.77.clone.1), dimensions={} | broadcast | bytes 8388610 | tf_op jit(solution)/shard_map/broadcast_in_dim | solution.py:15
  67.0 1.5 constant_dynamic-update-slice_fusion.3
  68.5 0.1 broadcast_bitcast_fusion
  68.5 3.1 %constant_dynamic-update-slice_fusion.2 = bf16[1024,4096]{0,1:T(8,128)(2,1)} fusion(bf16[1024,4096]{0,1:T(8,128)(2,1)} %constant_dynamic-update-slice_fusion.3, bf16[1024,1024]{0,1:T(8,128)(2,1)} %collective-permute-done, s32[]{:T(128)S(6)} %select_n.68), kind=kLoop, calls=%fused_computation.20 | loop fusion | bytes 4194308 | tf_op jit(solution)/shard_map/dynamic_update_slice | solution.py:25
  71.6 0.0 collective-permute-done.1
  71.6 3.1 %constant_dynamic-update-slice_fusion.1 = bf16[1024,4096]{0,1:T(8,128)(2,1)} fusion(bf16[1024,4096]{0,1:T(8,128)(2,1)} %constant_dynamic-update-slice_fusion.2, bf16[1024,1024]{0,1:T(8,128)(2,1)} %collective-permute-done.1, s32[]{:T(128)S(6)} %select_n.70), kind=kLoop, calls=%fused_computation.19 | loop fusion | bytes 4194308 | tf_op jit(solution)/shard_map/dynamic_update_slice | solution.py:32
  74.7 29.0 %collective-permute-done.2 = bf16[1024,1024]{0,1:T(8,128)(2,1)} collective-permute-done((bf16[1024,1024]{0,1:T(8,128)(2,1)}, bf16[1024,1024]{0,1:T(8,128)(2,1)}, u32[]{:S(2)}, u32[]{:S(2)}) %collective-permute-start.2) | collective-permute-done | bytes 2097184 | tf_op jit(solution)/shard_map/ppermute | solution.py:24
  103.7 3.1 %constant_dynamic-update-slice_fusion = bf16[1024,4096]{0,1:T(8,128)(2,1)} fusion(bf16[1024,4096]{0,1:T(8,128)(2,1)} %constant_dynamic-update-slice_fusion.1, bf16[1024,1024]{0,1:T(8,128)(2,1)} %collective-permute-done.2, s32[]{:T(128)S(6)} %select_n.72), kind=kLoop, calls=%fused_computation.18 | loop fusion | bytes 4194308 | tf_op jit(solution)/shard_map/dynamic_update_slice | solution.py:25
  106.8 11.7 %copy.18 = bf16[1024,32,128]{2,0,1:T(8,128)(2,1)} copy(bf16[1024,32,128]{0,2,1:T(8,128)(2,1)} %bitcast.1) | data formatting | bytes 16777216 | tf_op jit(solution)/shard_map/reshape | solution.py:56
  118.5 8.4 %gather_fusion = bf16[32,1024,128]{2,1,0:T(8,128)(2,1)} fusion(bf16[1024,32,128]{2,0,1:T(8,128)(2,1)} %copy.18, s32[1024]{0:T(1024)S(1)} %get-tuple-element.12), kind=kCustom, calls=%fused_computation | custom fusion | bytes 16777344 | tf_op jit(solution)/shard_map/jit(_take)/gather | solution.py:56
  126.9 11.8 %copy.19 = bf16[1024,32,128]{0,2,1:T(8,128)(2,1)} copy(bf16[1024,32,128]{2,0,1:T(8,128)(2,1)} %bitcast.12) | data formatting | bytes 16777216 | tf_op jit(solution)/shard_map/jit(_take)/gather | solution.py:56
  138.7 7.3 %bitcast_select_fusion = bf16[1024,4096]{0,1:T(8,128)(2,1)} fusion(bf16[1024,32,128]{0,2,1:T(8,128)(2,1)} %copy.19, pred[4096]{0:T(1024)(128)(4,1)S(1)} %broadcast_bitcast_fusion), kind=kLoop, calls=%fused_computation.6 | loop fusion | flops 4194304 | bytes 16781312 | tf_op jit(solution)/shard_map/jit(_take)/select_n | solution.py:56
  146.0 0.0 all-gather.2.cloned.1.call-done
  146.0 0.0 copy-start.2
  146.0 1.1 mul.37
  147.2 2.2 %copy-done.2 = bf16[1024,4096]{0,1:T(8,128)(2,1)S(1)} copy-done((bf16[1024,4096]{0,1:T(8,128)(2,1)S(1)}, bf16[1024,4096]{0,1:T(8,128)(2,1)}, u32[]{:S(2)}) %copy-start.2) | copy-done | bytes 8388632
  149.4 0.0 copy-start.1
  149.4 12.9 %fusion = f32[1024,1024]{1,0:T(8,128)} fusion(bf16[1024,4096]{0,1:T(8,128)(2,1)S(1)} %copy-done.2, bf16[4096,1024]{1,0:T(8,128)(2,1)} %all-gather.2.cloned.1.call-done, bf16[512,8,8,128]{3,2,1,0:T(8,128)(2,1)S(1)} %bitcast.13), kind=kOutput, calls=%fused_computation.4 | convolution fusion | flops 8594128896 | bytes 29360128 | tf_op jit(solution)/shard_map/dot_general | solution.py:57
  162.3 0.0 reduce-scatter.2.cloned.1.call-update
  162.3 22.8 %reduce-scatter.2.cloned.1.call-done = f32[1024,512]{1,0:T(8,128)} async-done(((f32[1024,1024]{1,0:T(8,128)}), f32[1024,512]{1,0:T(8,128)}) %reduce-scatter.2.cloned.1.call-update) | async-done | bytes 2097168 | tf_op jit(solution)/shard_map/reduce_scatter | solution.py:58
  185.1 2.7 %convert_element_type.11 = bf16[1024,512]{1,0:T(8,128)(2,1)} convert(f32[1024,512]{1,0:T(8,128)} %reduce-scatter.2.cloned.1.call-done) | non-fusion elementwise | flops 524288 | bytes 3145728 | tf_op jit(solution)/shard_map/convert_element_type | solution.py:58
  187.8 0.0 copy-done.1
  (3 shorter events, 0.0 us)
Async XLA Ops:
  6.5 52.3 %copy-start = (s32[64,32]{0,1:T(8,128)S(1)}, s32[64,32]{0,1:T(8,128)}, u32[]{:S(2)}) copy-start(s32[64,32]{0,1:T(8,128)} %param.8) | copy-start | bytes 24580
  6.5 139.5 %all-gather.2.cloned.1.call-start = ((), (), s32[]{:S(2)}) async-start(), calls=%async_computation.1 | async-start | bytes 8650752 | tf_op jit(solution)/shard_map/all_gather | solution.py:47
  7.3 177.9 %reduce-scatter.2.cloned.1.call-start = ((), (), s32[]{:S(2)}) async-start(), calls=%async_computation.2 | async-start | bytes 6291456 | tf_op jit(solution)/shard_map/reduce_scatter | solution.py:58
  10.2 47.1 %collective-permute-start = (bf16[1024,1024]{0,1:T(8,128)(2,1)S(1)}, bf16[1024,1024]{0,1:T(8,128)(2,1)}, u32[]{:S(2)}, u32[]{:S(2)}) collective-permute-start(bf16[1024,1024]{0,1:T(8,128)(2,1)S(1)} %copy.15), channel_id=1, source_target_pairs={{0,2},{2,4},{4,6},{6,0},{1,3},{3,5},{5,7},{7,1},{8,10},{10,12},{12... | collective-permute-start | bytes 6291464 | tf_op jit(solution)/shard_map/ppermute | solution.py:24
  12.4 59.3 %collective-permute-start.1 = (bf16[1024,1024]{0,1:T(8,128)(2,1)S(1)}, bf16[1024,1024]{0,1:T(8,128)(2,1)}, u32[]{:S(2)}, u32[]{:S(2)}) collective-permute-start(bf16[1024,1024]{0,1:T(8,128)(2,1)S(1)} %copy.15), channel_id=1, source_target_pairs={{0,6},{2,0},{4,2},{6,4},{1,7},{3,1},{5,3},{7,5},{8,14},{10,8},{12,... | collective-permute-start | bytes 6291464 | tf_op jit(solution)/shard_map/ppermute | solution.py:29
  57.3 46.4 %collective-permute-start.2 = (bf16[1024,1024]{0,1:T(8,128)(2,1)}, bf16[1024,1024]{0,1:T(8,128)(2,1)}, u32[]{:S(2)}, u32[]{:S(2)}) collective-permute-start(bf16[1024,1024]{0,1:T(8,128)(2,1)} %collective-permute-done), channel_id=1, source_target_pairs={{0,2},{2,4},{4,6},{6,0},{1,3},{3,5},{5,7},{7,1},{8,10},{10,12},{12... | collective-permute-start | bytes 6291464 | tf_op jit(solution)/shard_map/ppermute | solution.py:24
  146.0 3.4 %copy-start.2 = (bf16[1024,4096]{0,1:T(8,128)(2,1)S(1)}, bf16[1024,4096]{0,1:T(8,128)(2,1)}, u32[]{:S(2)}) copy-start(bf16[1024,4096]{0,1:T(8,128)(2,1)} %bitcast_select_fusion) | copy-start | bytes 25165828
  149.4 38.4 %copy-start.1 = (s32[64,32]{0,1:T(8,128)S(1)}, s32[64,32]{0,1:T(8,128)}, u32[]{:S(2)}) copy-start(s32[64,32]{0,1:T(8,128)} %param.8) | copy-start | bytes 24580
Sparse Core Ops, SparseCore 0:
  9.9 100.7 all-gather.1
  162.5 22.6 reduce-scatter.1
